TPU v7x, 32 devices: a whole 2x2x4 slice. The times are simulated.
32 devices in a mesh: ctx: 4 (over z), head: 4 (over y, x), seg: 2 (over core).
Axes of the slice: x: 2, y: 2, z: 4, core: 2. Of those that a mesh axis runs over, the one named last changes fastest.
Arguments:
- tokens_x: bfloat16 [4096, 2560], P(('ctx', 'seg'), 'head'), may hold values from -6 to 6
- gate_weight: bfloat16 [64, 3, 2560], P(None, None, 'head'), may hold values from -0.15625 to 0.15625
- queries: bfloat16 [4096, 64, 192], P(('ctx', 'seg'), 'head'), may hold values from -48 to 48
- keys: bfloat16 [4096, 4, 192], P(('ctx', 'seg'), 'head'), may hold values from -7 to 7
- values: bfloat16 [4096, 4, 128], P(('ctx', 'seg'), 'head'), may hold values from -24 to 24
- comp_key_weight: bfloat16 [4, 32, 192], P('head'), may hold values from -1 to 1
- comp_value_weight: bfloat16 [4, 32, 128], P('head'), may hold values from -1 to 1
- selected: int32 [32, 4, 16], P(('ctx', 'seg'), 'head'), may hold values from -1 to 63, as said below
Outputs:
- attention: bfloat16 [4096, 64, 128], P(('ctx', 'seg'), 'head')
Inputs may be any that keep to these rules, and one draw needn't show every extreme that they name: Each list names the tile's own fine blocks and block 0, then further blocks; live entries are distinct and at most the tile's last fine block; -1 marks an empty entry. For the tiles of one device (one block of 512 tokens) and one group, the blocks selected from the segment of 512 tokens of any other device number at most 1, and some device reaches it.
All inputs are finite; a program needn't handle non-finite values.
Results may differ from a plain program's by a relative error of at most 0.0059.
Values may be sent and summed in bfloat16 or wider, within the bound.
A program may use at most 128 MiB of HBM per device.

v0:
```python
import jax
import jax.numpy as jnp
from jax import lax
from jax.sharding import PartitionSpec as P

TILE = 128
BLK_S = 64
BLK_C = 32
NSEL = 16
WINDOW = 512


def shifted(value, axis, steps):
    count = lax.axis_size(axis)
    leading, last = (max(0, -steps), min(count, count - steps))
    return lax.ppermute(value, axis, [(source, source + steps) for source in range(leading, last)])


def attend(query, keys_part, values_part, allowed):
    scores = jnp.einsum(
        "rhd,kd->hrk", query, keys_part, preferred_element_type=jnp.float32
    ) * keys_part.shape[-1] ** (-0.5)
    scores = jnp.where(allowed[None], scores, -1e30)
    highest = jnp.max(scores, axis=-1, keepdims=True)
    weights = jnp.where(allowed[None], jnp.exp(scores - highest), 0.0)
    total = jnp.sum(weights, axis=-1)
    rounded = weights.astype(jnp.bfloat16)
    summed = jnp.einsum("hrk,kv->rhv", rounded, values_part, preferred_element_type=jnp.float32)
    return summed / jnp.maximum(total, 1.0).T[:, :, None]


def on_device(
    tokens_x, gate_weight, queries, keys, values, comp_key_weight, comp_value_weight, selected
):
    local_count = queries.shape[0]
    head_count = queries.shape[1]
    key_width = keys.shape[2]
    place = lax.axis_index(("ctx", "seg"))
    offset = place * local_count
    rows = gate_weight
    gates = jax.nn.sigmoid(
        lax.psum_scatter(
            jnp.einsum("hcd,td->hct", rows, tokens_x, preferred_element_type=jnp.float32),
            "head",
            scatter_dimension=0,
            tiled=True,
        )
    )
    own_keys = keys[:, 0]
    own_values = values[:, 0]
    packed = jnp.concatenate([own_keys, own_values], axis=1)
    coarse_local = local_count // BLK_C
    squeezed_keys = jnp.sum(
        own_keys.astype(jnp.float32).reshape(coarse_local, BLK_C, key_width)
        * comp_key_weight[0].astype(jnp.float32)[None],
        axis=1,
    )
    squeezed_values = jnp.sum(
        own_values.astype(jnp.float32).reshape(coarse_local, BLK_C, -1)
        * comp_value_weight[0].astype(jnp.float32)[None],
        axis=1,
    )
    coarse_packed = jnp.concatenate(
        [squeezed_keys.astype(jnp.bfloat16), squeezed_values.astype(jnp.bfloat16)], axis=1
    )
    coarse = lax.all_gather(coarse_packed, ("ctx", "seg"), axis=0, tiled=True)
    coarse_end = jnp.arange(coarse.shape[0], dtype=jnp.int32) * BLK_C + BLK_C - 1
    previous = shifted(packed, ("ctx", "seg"), 1)
    extended = jnp.concatenate([previous, packed], axis=0)
    chosen_all = selected[:, 0, :]
    blocks_all = jnp.maximum(chosen_all, 0)
    everything = lax.all_gather(packed, ("ctx", "seg"), axis=0, tiled=True)
    picked = everything.reshape(-1, BLK_S, packed.shape[1])[blocks_all]

    def one_tile(tile):
        begin = tile * TILE
        rows = offset + begin + jnp.arange(TILE, dtype=jnp.int32)
        query = lax.dynamic_slice_in_dim(queries, begin, TILE, 0)
        gate = lax.dynamic_slice_in_dim(gates, begin, TILE, 2)
        near = lax.dynamic_slice_in_dim(extended, begin + local_count - WINDOW, WINDOW + TILE, 0)
        near_pos = offset + begin - WINDOW + jnp.arange(WINDOW + TILE, dtype=jnp.int32)
        near_ok = (
            (near_pos[None, :] >= 0)
            & (near_pos[None, :] <= rows[:, None])
            & (near_pos[None, :] > rows[:, None] - WINDOW)
        )
        coarse_ok = coarse_end[None, :] <= rows[:, None]
        chosen = chosen_all[tile]
        blocks = jnp.maximum(chosen, 0)
        fine = picked[tile].reshape(NSEL * BLK_S, packed.shape[1])
        fine_pos = (blocks[:, None] * BLK_S + jnp.arange(BLK_S, dtype=jnp.int32)[None, :]).reshape(
            -1
        )
        live = jnp.repeat(chosen >= 0, BLK_S)
        fine_ok = live[None, :] & (fine_pos[None, :] <= rows[:, None])
        coarse_out = attend(query, coarse[:, :key_width], coarse[:, key_width:], coarse_ok)
        fine_out = attend(query, fine[:, :key_width], fine[:, key_width:], fine_ok)
        window_out = attend(query, near[:, :key_width], near[:, key_width:], near_ok)
        mixed = gate[:, 0, :].T[:, :, None] * coarse_out + gate[:, 1, :].T[:, :, None] * fine_out
        mixed = mixed + gate[:, 2, :].T[:, :, None] * window_out
        return mixed.astype(jnp.bfloat16)

    tiles = lax.map(one_tile, jnp.arange(local_count // TILE, dtype=jnp.int32))
    return tiles.reshape(local_count, head_count, -1)


def solution(mesh):
    in_specs = (
        P(("ctx", "seg"), "head"),
        P(None, None, "head"),
        P(("ctx", "seg"), "head", None),
        P(("ctx", "seg"), "head", None),
        P(("ctx", "seg"), "head", None),
        P("head", None, None),
        P("head", None, None),
        P(("ctx", "seg"), "head", None),
    )
    out_specs = P(("ctx", "seg"), "head", None)
    return jax.shard_map(
        on_device, mesh=mesh, in_specs=in_specs, out_specs=out_specs, check_vma=False
    )
```

profile of v0, /device:TPU:0, one launch (start us, length us, event | category | flops | bytes accessed | tf_op | source)
XLA Modules:
  0.0 226.0 jit_solution(13113540799511272979)
XLA Ops:
  8.5 2.1 fusion.86
  11.7 1.8 pad_maximum_fusion
  13.5 2.4 %collective-permute-start = (bf16[512,320]{1,0:T(8,128)(2,1)}, bf16[512,320]{1,0:T(8,128)(2,1)S(1)}, u32[]{:S(2)}, u32[]{:S(2)}) collective-permute-start(bf16[512,320]{1,0:T(8,128)(2,1)} %pad_maximum_fusion), channel_id=1, source_target_pairs={{0,1},{1,8},{8,9},{9,16},{16,17},{17,24},{24,25},{2,3},{3,10},{10,... | collective-permute-start | bytes 983048 | tf_op jit(solution)/shard_map/ppermute | solution.py:16
  16.2 15.6 %all_gather.6 = bf16[128,320]{1,0:T(8,128)(2,1)S(1)} all-gather(bf16[16,320]{1,0:T(8,128)(2,1)S(1)} %pad_maximum_fusion.1), channel_id=1, replica_groups=mesh['ctx'=4,'head'=4,'seg'=2] {'ctx','seg'}, dimensions={0}, use_global_device_ids=true | all-gather | bytes 92160 | tf_op jit(solution)/shard_map/all_gather | solution.py:66
  32.5 5.9 %reduce-scatter.2.cloned.1.call-done = f32[16,3,512]{2,0,1:T(8,128)} async-done(((f32[64,3,512]{2,0,1:T(8,128)}), f32[16,3,512]{2,0,1:T(8,128)}) %reduce-scatter.2.cloned.1.call-update) | async-done | bytes 98320 | tf_op jit(solution)/shard_map/reduce_scatter | solution.py:42
  39.4 15.5 %all-gather.2.cloned.1.call-done = bf16[4096,320]{1,0:T(8,128)(2,1)} async-done(((bf16[512,320]{1,0:T(8,128)(2,1)}), bf16[4096,320]{1,0:T(8,128)(2,1)}) %all-gather.2.cloned.1.call-update) | async-done | bytes 2621456 | tf_op jit(solution)/shard_map/all_gather | solution.py:72
  54.9 4.5 %gather_fusion = bf16[64,64,320]{2,1,0:T(8,128)(2,1)} fusion(bf16[64,64,320]{2,1,0:T(8,128)(2,1)} %bitcast.193, s32[1024]{0:T(1024)S(1)} %pad_clamp_fusion), kind=kCustom, calls=%fused_computation | custom fusion | bytes 5243136 | tf_op jit(solution)/shard_map/gather | solution.py:73
  59.4 159.2 %while.16 = (s32[]{:T(128)}, bf16[4,128,16,128]{3,2,1,0:T(8,128)(2,1)}, s32[4]{0:T(128)S(1)}, f32[16,3,512]{2,0,1:T(8,128)S(1)}, s32[]{:T(128)}, /*index=5*/bf16...) while((s32[]{:T(128)}, ...), condition=%wide.region_10.11_spmd.clone, body=%wide.region_3.10_spmd.clone.sunk | while | flops 2376428544 | bytes 36854732 | solution.py:103
  60.8 4.3 %fusion.126 = f32[640,128,16]{1,0,2:T(8,128)} fusion(bf16[512,16,192]{0,2,1:T(8,128)(2,1)} %get-tuple-element.459, s32[]{:T(128)S(6)} %select_n.150, bf16[1024,320]{0,1:T(8,128)(2,1)S(1)} %get-tuple-element.463, s32[]{:T(128)S(6)} %select_n.151), kind=kOutput, calls=%fused_computation.46.clone.1 | convolution fusion | flops 503316480 | bytes 6275080 | tf_op jit(solution)/shard_map/while/body/eval_jaxpr/rhd,kd->hrk/dot_general | solution.py:20
  65.4 8.3 %fusion.127 = (f32[16,128]{1,0:T(8,128)S(1)}, bf16[16,128,640]{1,2,0:T(8,128)(2,1)}) fusion(f32[640,128,16]{1,0,2:T(8,128)} %fusion.126, pred[128,640]{0,1:T(8,128)(4,1)S(1)} %compare_and_fusion.4), kind=kOutput, calls=%fused_computation.103.clone.1 | output fusion | flops 10486399 | bytes 7954432 | tf_op jit(solution)/shard_map/while/body/eval_jaxpr/sub | solution.py:25
  73.7 4.0 %fusion.128 = f32[128,16,128]{2,0,1:T(8,128)} fusion(bf16[16,128,640]{1,2,0:T(8,128)(2,1)} %get-tuple-element.405, f32[128,16]{0,1:T(8,128)S(1)} %maximum_bitcast_fusion.6, f32[128,16]{0,1:T(8,128)S(1)} %get-tuple-element.407, bf16[1024,320]{0,1:T(8,128)(2,1)S(1)} %get-tuple-element.463, s32[]{:T(128)S(6)} %select_n.151, s32[]{:T(128)S(6)} %add.284), kind=kOutput, calls=%fused_computation.36.clone.1 | convolution fusion | flops 336068608 | bytes 3850248 | tf_op jit(solution)/shard_map/while/body/eval_jaxpr/hrk,kv->rhv/dot_general | solution.py:28
  81.7 6.9 %fusion.129 = (f32[16,128]{1,0:T(8,128)S(1)}, bf16[16,128,1024]{1,2,0:T(8,128)(2,1)}) fusion(pred[128,1024]{0,1:T(8,128)(4,1)S(1)} %compare_and_fusion.5, bf16[512,16,192]{0,2,1:T(8,128)(2,1)} %get-tuple-element.459, s32[]{:T(128)S(6)} %select_n.150, bf16[1024,320]{1,0:T(8,128)(2,1)S(1)} %bitcast.187), kind=kOutput, calls=%fused_computation.104.clone.1 | convolution fusion | flops 817890304 | bytes 5775364 | tf_op jit(solution)/shard_map/while/body/eval_jaxpr/sub | solution.py:25
  88.5 5.4 %fusion.130 = f32[128,16,128]{2,0,1:T(8,128)} fusion(bf16[16,128,1024]{1,2,0:T(8,128)(2,1)} %get-tuple-element.408, f32[128,16]{0,1:T(8,128)S(1)} %maximum_bitcast_fusion.7, f32[128,16]{0,1:T(8,128)S(1)} %get-tuple-element.410, bf16[1024,320]{1,0:T(8,128)(2,1)S(1)} %bitcast.188), kind=kOutput, calls=%fused_computation.37.clone.1 | convolution fusion | flops 537395200 | bytes 5521408 | tf_op jit(solution)/shard_map/while/body/eval_jaxpr/hrk,kv->rhv/dot_general | solution.py:28
  95.9 2.1 fusion.132
  100.5 4.3 %fusion.126 = f32[640,128,16]{1,0,2:T(8,128)} fusion(bf16[512,16,192]{0,2,1:T(8,128)(2,1)} %get-tuple-element.459, s32[]{:T(128)S(6)} %select_n.150, bf16[1024,320]{0,1:T(8,128)(2,1)S(1)} %get-tuple-element.463, s32[]{:T(128)S(6)} %select_n.151), kind=kOutput, calls=%fused_computation.46.clone.1 | convolution fusion | flops 503316480 | bytes 6275080 | tf_op jit(solution)/shard_map/while/body/eval_jaxpr/rhd,kd->hrk/dot_general | solution.py:20
  105.1 8.3 %fusion.127 = (f32[16,128]{1,0:T(8,128)S(1)}, bf16[16,128,640]{1,2,0:T(8,128)(2,1)}) fusion(f32[640,128,16]{1,0,2:T(8,128)} %fusion.126, pred[128,640]{0,1:T(8,128)(4,1)S(1)} %compare_and_fusion.4), kind=kOutput, calls=%fused_computation.103.clone.1 | output fusion | flops 10486399 | bytes 7954432 | tf_op jit(solution)/shard_map/while/body/eval_jaxpr/sub | solution.py:25
  113.5 4.0 %fusion.128 = f32[128,16,128]{2,0,1:T(8,128)} fusion(bf16[16,128,640]{1,2,0:T(8,128)(2,1)} %get-tuple-element.405, f32[128,16]{0,1:T(8,128)S(1)} %maximum_bitcast_fusion.6, f32[128,16]{0,1:T(8,128)S(1)} %get-tuple-element.407, bf16[1024,320]{0,1:T(8,128)(2,1)S(1)} %get-tuple-element.463, s32[]{:T(128)S(6)} %select_n.151, s32[]{:T(128)S(6)} %add.284), kind=kOutput, calls=%fused_computation.36.clone.1 | convolution fusion | flops 336068608 | bytes 3850248 | tf_op jit(solution)/shard_map/while/body/eval_jaxpr/hrk,kv->rhv/dot_general | solution.py:28
  121.4 6.9 %fusion.129 = (f32[16,128]{1,0:T(8,128)S(1)}, bf16[16,128,1024]{1,2,0:T(8,128)(2,1)}) fusion(pred[128,1024]{0,1:T(8,128)(4,1)S(1)} %compare_and_fusion.5, bf16[512,16,192]{0,2,1:T(8,128)(2,1)} %get-tuple-element.459, s32[]{:T(128)S(6)} %select_n.150, bf16[1024,320]{1,0:T(8,128)(2,1)S(1)} %bitcast.187), kind=kOutput, calls=%fused_computation.104.clone.1 | convolution fusion | flops 817890304 | bytes 5775364 | tf_op jit(solution)/shard_map/while/body/eval_jaxpr/sub | solution.py:25
  128.3 5.4 %fusion.130 = f32[128,16,128]{2,0,1:T(8,128)} fusion(bf16[16,128,1024]{1,2,0:T(8,128)(2,1)} %get-tuple-element.408, f32[128,16]{0,1:T(8,128)S(1)} %maximum_bitcast_fusion.7, f32[128,16]{0,1:T(8,128)S(1)} %get-tuple-element.410, bf16[1024,320]{1,0:T(8,128)(2,1)S(1)} %bitcast.188), kind=kOutput, calls=%fused_computation.37.clone.1 | convolution fusion | flops 537395200 | bytes 5521408 | tf_op jit(solution)/shard_map/while/body/eval_jaxpr/hrk,kv->rhv/dot_general | solution.py:28
  135.7 2.1 fusion.132
  140.3 4.3 %fusion.126 = f32[640,128,16]{1,0,2:T(8,128)} fusion(bf16[512,16,192]{0,2,1:T(8,128)(2,1)} %get-tuple-element.459, s32[]{:T(128)S(6)} %select_n.150, bf16[1024,320]{0,1:T(8,128)(2,1)S(1)} %get-tuple-element.463, s32[]{:T(128)S(6)} %select_n.151), kind=kOutput, calls=%fused_computation.46.clone.1 | convolution fusion | flops 503316480 | bytes 6275080 | tf_op jit(solution)/shard_map/while/body/eval_jaxpr/rhd,kd->hrk/dot_general | solution.py:20
  144.9 8.3 %fusion.127 = (f32[16,128]{1,0:T(8,128)S(1)}, bf16[16,128,640]{1,2,0:T(8,128)(2,1)}) fusion(f32[640,128,16]{1,0,2:T(8,128)} %fusion.126, pred[128,640]{0,1:T(8,128)(4,1)S(1)} %compare_and_fusion.4), kind=kOutput, calls=%fused_computation.103.clone.1 | output fusion | flops 10486399 | bytes 7954432 | tf_op jit(solution)/shard_map/while/body/eval_jaxpr/sub | solution.py:25
  153.3 4.0 %fusion.128 = f32[128,16,128]{2,0,1:T(8,128)} fusion(bf16[16,128,640]{1,2,0:T(8,128)(2,1)} %get-tuple-element.405, f32[128,16]{0,1:T(8,128)S(1)} %maximum_bitcast_fusion.6, f32[128,16]{0,1:T(8,128)S(1)} %get-tuple-element.407, bf16[1024,320]{0,1:T(8,128)(2,1)S(1)} %get-tuple-element.463, s32[]{:T(128)S(6)} %select_n.151, s32[]{:T(128)S(6)} %add.284), kind=kOutput, calls=%fused_computation.36.clone.1 | convolution fusion | flops 336068608 | bytes 3850248 | tf_op jit(solution)/shard_map/while/body/eval_jaxpr/hrk,kv->rhv/dot_general | solution.py:28
  161.3 6.9 %fusion.129 = (f32[16,128]{1,0:T(8,128)S(1)}, bf16[16,128,1024]{1,2,0:T(8,128)(2,1)}) fusion(pred[128,1024]{0,1:T(8,128)(4,1)S(1)} %compare_and_fusion.5, bf16[512,16,192]{0,2,1:T(8,128)(2,1)} %get-tuple-element.459, s32[]{:T(128)S(6)} %select_n.150, bf16[1024,320]{1,0:T(8,128)(2,1)S(1)} %bitcast.187), kind=kOutput, calls=%fused_computation.104.clone.1 | convolution fusion | flops 817890304 | bytes 5775364 | tf_op jit(solution)/shard_map/while/body/eval_jaxpr/sub | solution.py:25
  168.1 5.4 %fusion.130 = f32[128,16,128]{2,0,1:T(8,128)} fusion(bf16[16,128,1024]{1,2,0:T(8,128)(2,1)} %get-tuple-element.408, f32[128,16]{0,1:T(8,128)S(1)} %maximum_bitcast_fusion.7, f32[128,16]{0,1:T(8,128)S(1)} %get-tuple-element.410, bf16[1024,320]{1,0:T(8,128)(2,1)S(1)} %bitcast.188), kind=kOutput, calls=%fused_computation.37.clone.1 | convolution fusion | flops 537395200 | bytes 5521408 | tf_op jit(solution)/shard_map/while/body/eval_jaxpr/hrk,kv->rhv/dot_general | solution.py:28
  175.5 2.1 fusion.132
  180.1 4.3 %fusion.126 = f32[640,128,16]{1,0,2:T(8,128)} fusion(bf16[512,16,192]{0,2,1:T(8,128)(2,1)} %get-tuple-element.459, s32[]{:T(128)S(6)} %select_n.150, bf16[1024,320]{0,1:T(8,128)(2,1)S(1)} %get-tuple-element.463, s32[]{:T(128)S(6)} %select_n.151), kind=kOutput, calls=%fused_computation.46.clone.1 | convolution fusion | flops 503316480 | bytes 6275080 | tf_op jit(solution)/shard_map/while/body/eval_jaxpr/rhd,kd->hrk/dot_general | solution.py:20
  184.8 8.3 %fusion.127 = (f32[16,128]{1,0:T(8,128)S(1)}, bf16[16,128,640]{1,2,0:T(8,128)(2,1)}) fusion(f32[640,128,16]{1,0,2:T(8,128)} %fusion.126, pred[128,640]{0,1:T(8,128)(4,1)S(1)} %compare_and_fusion.4), kind=kOutput, calls=%fused_computation.103.clone.1 | output fusion | flops 10486399 | bytes 7954432 | tf_op jit(solution)/shard_map/while/body/eval_jaxpr/sub | solution.py:25
  193.1 4.0 %fusion.128 = f32[128,16,128]{2,0,1:T(8,128)} fusion(bf16[16,128,640]{1,2,0:T(8,128)(2,1)} %get-tuple-element.405, f32[128,16]{0,1:T(8,128)S(1)} %maximum_bitcast_fusion.6, f32[128,16]{0,1:T(8,128)S(1)} %get-tuple-element.407, bf16[1024,320]{0,1:T(8,128)(2,1)S(1)} %get-tuple-element.463, s32[]{:T(128)S(6)} %select_n.151, s32[]{:T(128)S(6)} %add.284), kind=kOutput, calls=%fused_computation.36.clone.1 | convolution fusion | flops 336068608 | bytes 3850248 | tf_op jit(solution)/shard_map/while/body/eval_jaxpr/hrk,kv->rhv/dot_general | solution.py:28
  201.1 6.9 %fusion.129 = (f32[16,128]{1,0:T(8,128)S(1)}, bf16[16,128,1024]{1,2,0:T(8,128)(2,1)}) fusion(pred[128,1024]{0,1:T(8,128)(4,1)S(1)} %compare_and_fusion.5, bf16[512,16,192]{0,2,1:T(8,128)(2,1)} %get-tuple-element.459, s32[]{:T(128)S(6)} %select_n.150, bf16[1024,320]{1,0:T(8,128)(2,1)S(1)} %bitcast.187), kind=kOutput, calls=%fused_computation.104.clone.1 | convolution fusion | flops 817890304 | bytes 5775364 | tf_op jit(solution)/shard_map/while/body/eval_jaxpr/sub | solution.py:25
  207.9 5.4 %fusion.130 = f32[128,16,128]{2,0,1:T(8,128)} fusion(bf16[16,128,1024]{1,2,0:T(8,128)(2,1)} %get-tuple-element.408, f32[128,16]{0,1:T(8,128)S(1)} %maximum_bitcast_fusion.7, f32[128,16]{0,1:T(8,128)S(1)} %get-tuple-element.410, bf16[1024,320]{1,0:T(8,128)(2,1)S(1)} %bitcast.188), kind=kOutput, calls=%fused_computation.37.clone.1 | convolution fusion | flops 537395200 | bytes 5521408 | tf_op jit(solution)/shard_map/while/body/eval_jaxpr/hrk,kv->rhv/dot_general | solution.py:28
  215.3 2.1 fusion.132
  (118 shorter events, 27.6 us)
Async XLA Ops:
  7.4 1.1 copy-start
  7.4 8.6 %copy-start.1 = (bf16[512,1,128]{2,0,1:T(8,128)(2,1)S(1)}, bf16[512,1,128]{2,0,1:T(8,128)(2,1)}, u32[]{:S(2)}) copy-start(bf16[512,1,128]{2,0,1:T(8,128)(2,1)} %param.14) | copy-start | bytes 393220
  7.4 8.6 %copy-start.3 = (bf16[1,32,128]{2,1,0:T(8,128)(2,1)S(1)}, bf16[1,32,128]{2,1,0:T(8,128)(2,1)}, u32[]{:S(2)}) copy-start(bf16[1,32,128]{2,1,0:T(8,128)(2,1)} %param.16) | copy-start | bytes 24580
  7.4 8.7 %copy-start.2 = (bf16[1,32,192]{2,1,0:T(8,128)(2,1)S(1)}, bf16[1,32,192]{2,1,0:T(8,128)(2,1)}, u32[]{:S(2)}) copy-start(bf16[1,32,192]{2,1,0:T(8,128)(2,1)} %param.15) | copy-start | bytes 36868
  7.4 24.6 %copy-start.4 = (s32[4,1,16]{2,1,0:T(1,128)S(1)}, s32[4,1,16]{2,1,0:T(1,128)}, u32[]{:S(2)}) copy-start(s32[4,1,16]{2,1,0:T(1,128)} %param.17) | copy-start | bytes 772
  7.4 31.1 %reduce-scatter.2.cloned.1.call-start = ((), (), s32[]{:S(2)}) async-start(), calls=%async_computation.1 | async-start | bytes 491520 | tf_op jit(solution)/shard_map/reduce_scatter | solution.py:42
  10.6 44.3 %all-gather.2.cloned.1.call-start = ((), (), s32[]{:S(2)}) async-start(), calls=%async_computation.2 | async-start | bytes 3538944 | tf_op jit(solution)/shard_map/all_gather | solution.py:72
  13.5 18.6 %collective-permute-start = (bf16[512,320]{1,0:T(8,128)(2,1)}, bf16[512,320]{1,0:T(8,128)(2,1)S(1)}, u32[]{:S(2)}, u32[]{:S(2)}) collective-permute-start(bf16[512,320]{1,0:T(8,128)(2,1)} %pad_maximum_fusion), channel_id=1, source_target_pairs={{0,1},{1,8},{8,9},{9,16},{16,17},{17,24},{24,25},{2,3},{3,10},{10,... | collective-permute-start | bytes 983048 | tf_op jit(solution)/shard_map/ppermute | solution.py:16
Sparse Core Ops, SparseCore 0:
  11.0 27.4 reduce-scatter.1
Sparse Core Ops, SparseCore 1:
  13.6 41.2 all-gather.1
where the time goes:
time: 228 us; the launch traced here: 226 us
  matrix products  100 us (44%)
  other arithmetic  39.5 us (17%)
  waiting for transfers between devices  21.5 us (9%)
  local copies, waits for them, and re-layouts  20.6 us (9%)
  blocking collectives  15.6 us (7%)
  between operations  15 us (7%)
  loops' own time  11.2 us (5%)
  starting transfers between devices  2.5 us (1%)
    dot_general x12, matrix products, attend(): jnp.einsum('hrk,kv->rhv', rounded, values_part, preferred_element_type=jn...  46.3 us
    sub x8, matrix products, attend(): weights = jnp.where(allowed[None], jnp.exp(scores - highest), 0.0)  34.5 us
    sub x4, other arithmetic, attend(): weights = jnp.where(allowed[None], jnp.exp(scores - highest), 0.0)  33.2 us
    dot_general x4, matrix products, attend(): jnp.einsum('rhd,kd->hrk', query, keys_part, preferred_element_type=jnp.fl...  17.4 us
    all_gather x1, blocking collectives, on_device(): coarse = lax.all_gather(coarse_packed, ('ctx', 'seg'), axis=0, tiled=True)  15.6 us
    all_gather x1, waiting for transfers between devices, on_device(): everything = lax.all_gather(packed, ('ctx', 'seg'), axis=0, tiled=True)  15.5 us
    another operation x1, loops' own time, on_device(): tiles = lax.map(one_tile, jnp.arange(local_count // TILE, dtype=jnp.int32))  11.2 us
    reduce_scatter x1, waiting for transfers between devices, on_device(): lax.psum_scatter(jnp.einsum('hcd,td->hct', rows, tokens_x, preferred_elem...  5.93 us
  transfers between devices with their start and end apart: 3, of which 2 were waited for; matrix products, arithmetic and copies ran while one was open for 2% of the time, Pallas kernels for 0%

commit v1 on v0

--- a/solution.py
+++ b/solution.py
@@ -69,7 +69,10 @@
     extended = jnp.concatenate([previous, packed], axis=0)
     chosen_all = selected[:, 0, :]
     blocks_all = jnp.maximum(chosen_all, 0)
-    everything = lax.all_gather(packed, ("ctx", "seg"), axis=0, tiled=True)
+    everything = jnp.concatenate(
+        lax.all_to_all(jnp.stack([packed] * lax.axis_size(("ctx", "seg"))), ("ctx", "seg"), 0, 0),
+        axis=0,
+    )
     picked = everything.reshape(-1, BLK_S, packed.shape[1])[blocks_all]
 
     def one_tile(tile):

time: 228 us -> 270 us (1.18)
  blocking collectives: 15.6 us -> 61.1 us
  waiting for transfers between devices: 21.5 us -> 0.02 us
  starting transfers between devices: 2.5 us -> 9.63 us
  local copies, waits for them, and re-layouts: 20.6 us -> 27.6 us
  other arithmetic: 39.5 us -> 44.8 us
    all_gather x1, blocking collectives: 15.6 us -> 61.1 us  [on_device(): coarse = lax.all_gather(coarse_packed, ('ctx', 'seg'), axis=0, tiled=True)]
    all_gather x1 -> x0, waiting for transfers between devices: 15.5 us -> none  [on_device(): everything = lax.all_gather(packed, ('ctx', 'seg'), axis=0, tiled=True)]
    all_to_all x0 -> x1, starting transfers between devices: none -> 6.5 us  [on_device(): lax.all_to_all(jnp.stack([packed] * lax.axis_size(('ctx', 'seg'))), ('ctx...]
    reduce_scatter x1, waiting for transfers between devices: 5.93 us -> 0.01 us  [on_device(): lax.psum_scatter(jnp.einsum('hcd,td->hct', rows, tokens_x, preferred_elem...]
    all_to_all x0 -> x1, local copies, waits for them, and re-layouts: none -> 2.79 us  [on_device(): lax.all_to_all(jnp.stack([packed] * lax.axis_size(('ctx', 'seg'))), ('ctx...]
  transfers between devices with their start and end apart: 3 -> 3, of which waited for: 2 -> 0; matrix products, arithmetic and copies ran while one was open for 2% -> 5% of each run, Pallas kernels for 0% -> 0%
where the time goes in v1:
time: 270 us; the launch traced here: 268 us
  matrix products  100 us (37%)
  blocking collectives  61.1 us (23%)
  other arithmetic  44.8 us (17%)
  local copies, waits for them, and re-layouts  27.6 us (10%)
  between operations  13.5 us (5%)
  loops' own time  11.4 us (4%)
  starting transfers between devices  9.63 us (4%)
    all_gather x1, blocking collectives, on_device(): coarse = lax.all_gather(coarse_packed, ('ctx', 'seg'), axis=0, tiled=True)  61.1 us
    dot_general x12, matrix products, attend(): jnp.einsum('hrk,kv->rhv', rounded, values_part, preferred_element_type=jn...  46.3 us
    sub x8, matrix products, attend(): weights = jnp.where(allowed[None], jnp.exp(scores - highest), 0.0)  34.5 us
    sub x4, other arithmetic, attend(): weights = jnp.where(allowed[None], jnp.exp(scores - highest), 0.0)  33.2 us
    dot_general x4, matrix products, attend(): jnp.einsum('rhd,kd->hrk', query, keys_part, preferred_element_type=jnp.fl...  17.4 us
    another operation x1, loops' own time, on_device(): tiles = lax.map(one_tile, jnp.arange(local_count // TILE, dtype=jnp.int32))  11.4 us
    all_to_all x1, starting transfers between devices, on_device(): lax.all_to_all(jnp.stack([packed] * lax.axis_size(('ctx', 'seg'))), ('ctx...  6.5 us
  transfers between devices with their start and end apart: 3, of which 0 were waited for; matrix products, arithmetic and copies ran while one was open for 5% of the time, Pallas kernels for 0%

profile of v1, /device:TPU:0, one launch (start us, length us, event | category | flops | bytes accessed | tf_op | source)
XLA Modules:
  0.0 268.3 jit_solution(8002712552296288936)
XLA Ops:
  11.1 6.5 %all-to-all-start = ((bf16[8,512,320]{1,2,0:T(8,128)(2,1)}), bf16[8,512,320]{1,2,0:T(8,128)(2,1)S(1)}, u32[]{:S(2)}, u32[]{:S(2)}) async-start(bf16[8,512,320]{1,2,0:T(8,128)(2,1)} %stack.2), calls=%async_computation.1 | async-start | bytes 5242880 | tf_op jit(solution)/shard_map/all_to_all | solution.py:73
  17.6 3.1 %collective-permute-start = (bf16[512,320]{0,1:T(8,128)(2,1)}, bf16[512,320]{0,1:T(8,128)(2,1)}, u32[]{:S(2)}, u32[]{:S(2)}) collective-permute-start(bf16[512,320]{0,1:T(8,128)(2,1)} %copy-done.3), channel_id=1, source_target_pairs={{0,1},{1,8},{8,9},{9,16},{16,17},{17,24},{24,25},{2,3},{3,10},{10,... | collective-permute-start | bytes 983048 | tf_op jit(solution)/shard_map/ppermute | solution.py:16
  20.7 2.1 fusion.86
  25.8 61.1 %all_gather.3 = bf16[128,320]{1,0:T(8,128)(2,1)} all-gather(bf16[16,320]{1,0:T(8,128)(2,1)S(1)} %pad_maximum_fusion.1), channel_id=1, replica_groups=mesh['ctx'=4,'head'=4,'seg'=2] {'ctx','seg'}, dimensions={0}, use_global_device_ids=true | all-gather | bytes 92160 | tf_op jit(solution)/shard_map/all_gather | solution.py:66
  91.7 2.0 maximum_maximum_fusion
  94.6 2.8 %copy.53 = bf16[8,512,320]{2,1,0:T(8,128)(2,1)} copy(bf16[8,512,320]{1,2,0:T(8,128)(2,1)S(1)} %all-to-all-done) | data formatting | bytes 5242880 | tf_op jit(solution)/shard_map/all_to_all | solution.py:73
  97.4 4.6 %gather_fusion = bf16[64,64,320]{2,1,0:T(8,128)(2,1)} fusion(bf16[64,64,320]{2,1,0:T(8,128)(2,1)} %bitcast.190, s32[1024]{0:T(1024)S(1)} %copy-done.6), kind=kCustom, calls=%fused_computation | custom fusion | bytes 5243136 | tf_op jit(solution)/shard_map/gather | solution.py:76
  102.0 159.4 %while.16 = (s32[]{:T(128)}, bf16[4,128,16,128]{3,2,1,0:T(8,128)(2,1)}, s32[4]{0:T(128)S(1)}, f32[16,3,512]{2,0,1:T(8,128)S(1)}, s32[]{:T(128)}, /*index=5*/bf16...) while((s32[]{:T(128)}, ...), condition=%wide.region_10.11_spmd.clone, body=%wide.region_3.10_spmd.clone.sunk | while | flops 2376428544 | bytes 36854732 | solution.py:106
  103.6 4.3 %fusion.126 = f32[640,128,16]{1,0,2:T(8,128)} fusion(bf16[512,16,192]{0,2,1:T(8,128)(2,1)} %get-tuple-element.459, s32[]{:T(128)S(6)} %select_n.150, bf16[1024,320]{0,1:T(8,128)(2,1)S(1)} %get-tuple-element.463, s32[]{:T(128)S(6)} %select_n.151), kind=kOutput, calls=%fused_computation.46.clone.1 | convolution fusion | flops 503316480 | bytes 6275080 | tf_op jit(solution)/shard_map/while/body/eval_jaxpr/rhd,kd->hrk/dot_general | solution.py:20
  108.2 8.3 %fusion.127 = (f32[16,128]{1,0:T(8,128)S(1)}, bf16[16,128,640]{1,2,0:T(8,128)(2,1)}) fusion(f32[640,128,16]{1,0,2:T(8,128)} %fusion.126, pred[128,640]{0,1:T(8,128)(4,1)S(1)} %compare_and_fusion.4), kind=kOutput, calls=%fused_computation.103.clone.1 | output fusion | flops 10486399 | bytes 7954432 | tf_op jit(solution)/shard_map/while/body/eval_jaxpr/sub | solution.py:25
  116.5 4.0 %fusion.128 = f32[128,16,128]{2,0,1:T(8,128)} fusion(bf16[16,128,640]{1,2,0:T(8,128)(2,1)} %get-tuple-element.405, f32[128,16]{0,1:T(8,128)S(1)} %maximum_bitcast_fusion.6, f32[128,16]{0,1:T(8,128)S(1)} %get-tuple-element.407, bf16[1024,320]{0,1:T(8,128)(2,1)S(1)} %get-tuple-element.463, s32[]{:T(128)S(6)} %select_n.151, s32[]{:T(128)S(6)} %add.284), kind=kOutput, calls=%fused_computation.36.clone.1 | convolution fusion | flops 336068608 | bytes 3850248 | tf_op jit(solution)/shard_map/while/body/eval_jaxpr/hrk,kv->rhv/dot_general | solution.py:28
  124.5 6.9 %fusion.129 = (f32[16,128]{1,0:T(8,128)S(1)}, bf16[16,128,1024]{1,2,0:T(8,128)(2,1)}) fusion(pred[128,1024]{0,1:T(8,128)(4,1)S(1)} %compare_and_fusion.5, bf16[512,16,192]{0,2,1:T(8,128)(2,1)} %get-tuple-element.459, s32[]{:T(128)S(6)} %select_n.150, bf16[1024,320]{1,0:T(8,128)(2,1)S(1)} %bitcast.187), kind=kOutput, calls=%fused_computation.104.clone.1 | convolution fusion | flops 817890304 | bytes 5775364 | tf_op jit(solution)/shard_map/while/body/eval_jaxpr/sub | solution.py:25
  131.3 5.4 %fusion.130 = f32[128,16,128]{2,0,1:T(8,128)} fusion(bf16[16,128,1024]{1,2,0:T(8,128)(2,1)} %get-tuple-element.408, f32[128,16]{0,1:T(8,128)S(1)} %maximum_bitcast_fusion.7, f32[128,16]{0,1:T(8,128)S(1)} %get-tuple-element.410, bf16[1024,320]{1,0:T(8,128)(2,1)S(1)} %bitcast.188), kind=kOutput, calls=%fused_computation.37.clone.1 | convolution fusion | flops 537395200 | bytes 5521408 | tf_op jit(solution)/shard_map/while/body/eval_jaxpr/hrk,kv->rhv/dot_general | solution.py:28
  138.7 2.1 fusion.132
  143.4 4.3 %fusion.126 = f32[640,128,16]{1,0,2:T(8,128)} fusion(bf16[512,16,192]{0,2,1:T(8,128)(2,1)} %get-tuple-element.459, s32[]{:T(128)S(6)} %select_n.150, bf16[1024,320]{0,1:T(8,128)(2,1)S(1)} %get-tuple-element.463, s32[]{:T(128)S(6)} %select_n.151), kind=kOutput, calls=%fused_computation.46.clone.1 | convolution fusion | flops 503316480 | bytes 6275080 | tf_op jit(solution)/shard_map/while/body/eval_jaxpr/rhd,kd->hrk/dot_general | solution.py:20
  148.0 8.3 %fusion.127 = (f32[16,128]{1,0:T(8,128)S(1)}, bf16[16,128,640]{1,2,0:T(8,128)(2,1)}) fusion(f32[640,128,16]{1,0,2:T(8,128)} %fusion.126, pred[128,640]{0,1:T(8,128)(4,1)S(1)} %compare_and_fusion.4), kind=kOutput, calls=%fused_computation.103.clone.1 | output fusion | flops 10486399 | bytes 7954432 | tf_op jit(solution)/shard_map/while/body/eval_jaxpr/sub | solution.py:25
  156.3 4.0 %fusion.128 = f32[128,16,128]{2,0,1:T(8,128)} fusion(bf16[16,128,640]{1,2,0:T(8,128)(2,1)} %get-tuple-element.405, f32[128,16]{0,1:T(8,128)S(1)} %maximum_bitcast_fusion.6, f32[128,16]{0,1:T(8,128)S(1)} %get-tuple-element.407, bf16[1024,320]{0,1:T(8,128)(2,1)S(1)} %get-tuple-element.463, s32[]{:T(128)S(6)} %select_n.151, s32[]{:T(128)S(6)} %add.284), kind=kOutput, calls=%fused_computation.36.clone.1 | convolution fusion | flops 336068608 | bytes 3850248 | tf_op jit(solution)/shard_map/while/body/eval_jaxpr/hrk,kv->rhv/dot_general | solution.py:28
  164.3 6.9 %fusion.129 = (f32[16,128]{1,0:T(8,128)S(1)}, bf16[16,128,1024]{1,2,0:T(8,128)(2,1)}) fusion(pred[128,1024]{0,1:T(8,128)(4,1)S(1)} %compare_and_fusion.5, bf16[512,16,192]{0,2,1:T(8,128)(2,1)} %get-tuple-element.459, s32[]{:T(128)S(6)} %select_n.150, bf16[1024,320]{1,0:T(8,128)(2,1)S(1)} %bitcast.187), kind=kOutput, calls=%fused_computation.104.clone.1 | convolution fusion | flops 817890304 | bytes 5775364 | tf_op jit(solution)/shard_map/while/body/eval_jaxpr/sub | solution.py:25
  171.1 5.4 %fusion.130 = f32[128,16,128]{2,0,1:T(8,128)} fusion(bf16[16,128,1024]{1,2,0:T(8,128)(2,1)} %get-tuple-element.408, f32[128,16]{0,1:T(8,128)S(1)} %maximum_bitcast_fusion.7, f32[128,16]{0,1:T(8,128)S(1)} %get-tuple-element.410, bf16[1024,320]{1,0:T(8,128)(2,1)S(1)} %bitcast.188), kind=kOutput, calls=%fused_computation.37.clone.1 | convolution fusion | flops 537395200 | bytes 5521408 | tf_op jit(solution)/shard_map/while/body/eval_jaxpr/hrk,kv->rhv/dot_general | solution.py:28
  178.5 2.1 fusion.132
  183.1 4.3 %fusion.126 = f32[640,128,16]{1,0,2:T(8,128)} fusion(bf16[512,16,192]{0,2,1:T(8,128)(2,1)} %get-tuple-element.459, s32[]{:T(128)S(6)} %select_n.150, bf16[1024,320]{0,1:T(8,128)(2,1)S(1)} %get-tuple-element.463, s32[]{:T(128)S(6)} %select_n.151), kind=kOutput, calls=%fused_computation.46.clone.1 | convolution fusion | flops 503316480 | bytes 6275080 | tf_op jit(solution)/shard_map/while/body/eval_jaxpr/rhd,kd->hrk/dot_general | solution.py:20
  187.7 8.3 %fusion.127 = (f32[16,128]{1,0:T(8,128)S(1)}, bf16[16,128,640]{1,2,0:T(8,128)(2,1)}) fusion(f32[640,128,16]{1,0,2:T(8,128)} %fusion.126, pred[128,640]{0,1:T(8,128)(4,1)S(1)} %compare_and_fusion.4), kind=kOutput, calls=%fused_computation.103.clone.1 | output fusion | flops 10486399 | bytes 7954432 | tf_op jit(solution)/shard_map/while/body/eval_jaxpr/sub | solution.py:25
  196.1 4.0 %fusion.128 = f32[128,16,128]{2,0,1:T(8,128)} fusion(bf16[16,128,640]{1,2,0:T(8,128)(2,1)} %get-tuple-element.405, f32[128,16]{0,1:T(8,128)S(1)} %maximum_bitcast_fusion.6, f32[128,16]{0,1:T(8,128)S(1)} %get-tuple-element.407, bf16[1024,320]{0,1:T(8,128)(2,1)S(1)} %get-tuple-element.463, s32[]{:T(128)S(6)} %select_n.151, s32[]{:T(128)S(6)} %add.284), kind=kOutput, calls=%fused_computation.36.clone.1 | convolution fusion | flops 336068608 | bytes 3850248 | tf_op jit(solution)/shard_map/while/body/eval_jaxpr/hrk,kv->rhv/dot_general | solution.py:28
  204.1 6.9 %fusion.129 = (f32[16,128]{1,0:T(8,128)S(1)}, bf16[16,128,1024]{1,2,0:T(8,128)(2,1)}) fusion(pred[128,1024]{0,1:T(8,128)(4,1)S(1)} %compare_and_fusion.5, bf16[512,16,192]{0,2,1:T(8,128)(2,1)} %get-tuple-element.459, s32[]{:T(128)S(6)} %select_n.150, bf16[1024,320]{1,0:T(8,128)(2,1)S(1)} %bitcast.187), kind=kOutput, calls=%fused_computation.104.clone.1 | convolution fusion | flops 817890304 | bytes 5775364 | tf_op jit(solution)/shard_map/while/body/eval_jaxpr/sub | solution.py:25
  210.9 5.4 %fusion.130 = f32[128,16,128]{2,0,1:T(8,128)} fusion(bf16[16,128,1024]{1,2,0:T(8,128)(2,1)} %get-tuple-element.408, f32[128,16]{0,1:T(8,128)S(1)} %maximum_bitcast_fusion.7, f32[128,16]{0,1:T(8,128)S(1)} %get-tuple-element.410, bf16[1024,320]{1,0:T(8,128)(2,1)S(1)} %bitcast.188), kind=kOutput, calls=%fused_computation.37.clone.1 | convolution fusion | flops 537395200 | bytes 5521408 | tf_op jit(solution)/shard_map/while/body/eval_jaxpr/hrk,kv->rhv/dot_general | solution.py:28
  218.3 2.1 fusion.132
  222.9 4.3 %fusion.126 = f32[640,128,16]{1,0,2:T(8,128)} fusion(bf16[512,16,192]{0,2,1:T(8,128)(2,1)} %get-tuple-element.459, s32[]{:T(128)S(6)} %select_n.150, bf16[1024,320]{0,1:T(8,128)(2,1)S(1)} %get-tuple-element.463, s32[]{:T(128)S(6)} %select_n.151), kind=kOutput, calls=%fused_computation.46.clone.1 | convolution fusion | flops 503316480 | bytes 6275080 | tf_op jit(solution)/shard_map/while/body/eval_jaxpr/rhd,kd->hrk/dot_general | solution.py:20
  227.6 8.3 %fusion.127 = (f32[16,128]{1,0:T(8,128)S(1)}, bf16[16,128,640]{1,2,0:T(8,128)(2,1)}) fusion(f32[640,128,16]{1,0,2:T(8,128)} %fusion.126, pred[128,640]{0,1:T(8,128)(4,1)S(1)} %compare_and_fusion.4), kind=kOutput, calls=%fused_computation.103.clone.1 | output fusion | flops 10486399 | bytes 7954432 | tf_op jit(solution)/shard_map/while/body/eval_jaxpr/sub | solution.py:25
  235.9 4.0 %fusion.128 = f32[128,16,128]{2,0,1:T(8,128)} fusion(bf16[16,128,640]{1,2,0:T(8,128)(2,1)} %get-tuple-element.405, f32[128,16]{0,1:T(8,128)S(1)} %maximum_bitcast_fusion.6, f32[128,16]{0,1:T(8,128)S(1)} %get-tuple-element.407, bf16[1024,320]{0,1:T(8,128)(2,1)S(1)} %get-tuple-element.463, s32[]{:T(128)S(6)} %select_n.151, s32[]{:T(128)S(6)} %add.284), kind=kOutput, calls=%fused_computation.36.clone.1 | convolution fusion | flops 336068608 | bytes 3850248 | tf_op jit(solution)/shard_map/while/body/eval_jaxpr/hrk,kv->rhv/dot_general | solution.py:28
  243.9 6.9 %fusion.129 = (f32[16,128]{1,0:T(8,128)S(1)}, bf16[16,128,1024]{1,2,0:T(8,128)(2,1)}) fusion(pred[128,1024]{0,1:T(8,128)(4,1)S(1)} %compare_and_fusion.5, bf16[512,16,192]{0,2,1:T(8,128)(2,1)} %get-tuple-element.459, s32[]{:T(128)S(6)} %select_n.150, bf16[1024,320]{1,0:T(8,128)(2,1)S(1)} %bitcast.187), kind=kOutput, calls=%fused_computation.104.clone.1 | convolution fusion | flops 817890304 | bytes 5775364 | tf_op jit(solution)/shard_map/while/body/eval_jaxpr/sub | solution.py:25
  250.7 5.4 %fusion.130 = f32[128,16,128]{2,0,1:T(8,128)} fusion(bf16[16,128,1024]{1,2,0:T(8,128)(2,1)} %get-tuple-element.408, f32[128,16]{0,1:T(8,128)S(1)} %maximum_bitcast_fusion.7, f32[128,16]{0,1:T(8,128)S(1)} %get-tuple-element.410, bf16[1024,320]{1,0:T(8,128)(2,1)S(1)} %bitcast.188), kind=kOutput, calls=%fused_computation.37.clone.1 | convolution fusion | flops 537395200 | bytes 5521408 | tf_op jit(solution)/shard_map/while/body/eval_jaxpr/hrk,kv->rhv/dot_general | solution.py:28
  258.1 2.1 fusion.132
  (127 shorter events, 36.9 us)
Async XLA Ops:
  6.5 14.2 %copy-start = (bf16[512,640]{1,0:T(8,128)(2,1)S(1)}, bf16[512,640]{1,0:T(8,128)(2,1)}, u32[]{:S(2)}) copy-start(bf16[512,640]{1,0:T(8,128)(2,1)} %param.10) | copy-start | bytes 1966084
  7.6 3.5 %copy-start.4 = (bf16[512,1,128]{0,2,1:T(8,128)(2,1)}, bf16[512,1,128]{0,2,1:T(8,128)(2,1)S(1)}, u32[]{:S(2)}) copy-start(bf16[512,1,128]{0,2,1:T(8,128)(2,1)S(1)} %copy.52) | copy-start | bytes 393220
  8.6 0.7 copy-start.3
  11.1 11.7 %copy-start.5 = (bf16[1,32,192]{2,1,0:T(8,128)(2,1)S(1)}, bf16[1,32,192]{2,1,0:T(8,128)(2,1)}, u32[]{:S(2)}) copy-start(bf16[1,32,192]{2,1,0:T(8,128)(2,1)} %param.15) | copy-start | bytes 36868
  11.1 11.8 %copy-start.7 = (bf16[1,32,128]{2,1,0:T(8,128)(2,1)S(1)}, bf16[1,32,128]{2,1,0:T(8,128)(2,1)}, u32[]{:S(2)}) copy-start(bf16[1,32,128]{2,1,0:T(8,128)(2,1)} %param.16) | copy-start | bytes 24580
  11.1 11.8 %copy-start.2 = (bf16[512,1,192]{0,2,1:T(8,128)(2,1)S(1)}, bf16[512,1,192]{0,2,1:T(8,128)(2,1)}, u32[]{:S(2)}) copy-start(bf16[512,1,192]{0,2,1:T(8,128)(2,1)} %param.13) | copy-start | bytes 589828
  11.1 83.5 %all-to-all-start = ((bf16[8,512,320]{1,2,0:T(8,128)(2,1)}), bf16[8,512,320]{1,2,0:T(8,128)(2,1)S(1)}, u32[]{:S(2)}, u32[]{:S(2)}) async-start(bf16[8,512,320]{1,2,0:T(8,128)(2,1)} %stack.2), calls=%async_computation.1 | async-start | bytes 5242880 | tf_op jit(solution)/shard_map/all_to_all | solution.py:73
  17.6 76.1 %reduce-scatter.2.cloned.1.call-start = ((), (), s32[]{:S(2)}) async-start(), calls=%async_computation.2 | async-start | bytes 491520 | tf_op jit(solution)/shard_map/reduce_scatter | solution.py:42
  17.6 74.1 %collective-permute-start = (bf16[512,320]{0,1:T(8,128)(2,1)}, bf16[512,320]{0,1:T(8,128)(2,1)}, u32[]{:S(2)}, u32[]{:S(2)}) collective-permute-start(bf16[512,320]{0,1:T(8,128)(2,1)} %copy-done.3), channel_id=1, source_target_pairs={{0,1},{1,8},{8,9},{9,16},{16,17},{17,24},{24,25},{2,3},{3,10},{10,... | collective-permute-start | bytes 983048 | tf_op jit(solution)/shard_map/ppermute | solution.py:16
  93.7 3.7 %copy-start.6 = (s32[1024]{0:T(1024)S(1)}, s32[1024]{0:T(1024)}, u32[]{:S(2)}) copy-start(s32[1024]{0:T(1024)} %pad_clamp_fusion) | copy-start | bytes 12292
  97.4 4.6 %copy-start.1 = (bf16[1024,320]{0,1:T(8,128)(2,1)S(1)}, bf16[1024,320]{0,1:T(8,128)(2,1)}, u32[]{:S(2)}) copy-start(bf16[1024,320]{0,1:T(8,128)(2,1)} %maximum_maximum_fusion) | copy-start | bytes 1966084
  97.4 4.6 %copy-start.8 = (s32[4,1,16]{2,1,0:T(1,128)S(1)}, s32[4,1,16]{2,1,0:T(1,128)}, u32[]{:S(2)}) copy-start(s32[4,1,16]{2,1,0:T(1,128)} %param.17) | copy-start | bytes 772
Sparse Core Ops, SparseCore 0:
  23.0 25.2 reduce-scatter.1
